TPU v7x, 128 devices: a whole 4x4x4 slice. The times are simulated.
128 devices in a mesh: lat: 8 (over z_hi, x), lon: 16 (over y, z_lo, core).
Axes of the slice: x: 4, y: 4, z: 4 (z_hi: 2, z_lo: 2; z = z_hi * 2 + z_lo), core: 2. Of those that a mesh axis runs over, the one named last changes fastest.
Arguments:
- features: bfloat16 [128, 3072, 128], P('lat', 'lon'), may hold values from -6 to 6
- cotangent: bfloat16 [128, 3072, 128], P('lat', 'lon'), may hold values from -6 to 6
- w_first: bfloat16 [1152, 128], P(('lat', 'lon')), may hold values from -0.1875 to 0.1875
- w_second: bfloat16 [1152, 128], P(('lat', 'lon')), may hold values from -0.1875 to 0.1875
Outputs:
- grad_features: bfloat16 [128, 3072, 128], P('lat', 'lon')
- grad_first: float32 [1152, 128], P(('lat', 'lon'))
- grad_second: float32 [1152, 128], P(('lat', 'lon'))
All inputs are finite; a program needn't handle non-finite values.
Results may differ from a plain program's by a relative error of at most 0.0033.
Values may be sent and summed in bfloat16 or wider, within the bound.
No kernel may reach another device: no remote copies, remote signals or barrier semaphores. Data moves between devices by JAX's collectives and lax.ppermute only.
A program may use at most 64 MiB of HBM per device.

v0:
```python
import jax
import jax.numpy as jnp
from jax import lax
from jax.sharding import PartitionSpec as P


def padded_2(block, sides, width, periodic):
    for axis, dim in sides:
        count = lax.axis_size(axis)
        forward = [(i, i + 1) for i in range(count - 1)]
        if periodic:
            forward.append((count - 1, 0))
        backward = [(target, source) for source, target in forward]
        low = lax.ppermute(
            lax.slice_in_dim(block, block.shape[dim] - width, None, axis=dim), axis, forward
        )
        high = lax.ppermute(lax.slice_in_dim(block, 0, width, axis=dim), axis, backward)
        block = jnp.concatenate([low, block, high], axis=dim)
    return block


def add_rims(field, width):
    field = padded_2(field, (("lon", 1),), width, True)
    return padded_2(field, (("lat", 0),), width, False)


def forward_conv(padded, weight, rows, cols):
    chans = padded.shape[2]
    total = jnp.zeros((rows * cols, weight.shape[1]), jnp.float32)
    for tap in range(9):
        shift_r, shift_c = divmod(tap, 3)
        piece = padded[shift_r : shift_r + rows, shift_c : shift_c + cols].reshape(-1, chans)
        total = total + jnp.dot(
            piece, weight[tap * chans : (tap + 1) * chans], preferred_element_type=jnp.float32
        )
    return total.reshape(rows, cols, -1)


def transpose_conv(padded, weight, rows, cols):
    chans = weight.shape[1]
    inner = weight.shape[0] // 9
    total = jnp.zeros((rows * cols, inner), jnp.float32)
    for tap in range(9):
        shift_r, shift_c = divmod(tap, 3)
        piece = padded[2 - shift_r : 2 - shift_r + rows, 2 - shift_c : 2 - shift_c + cols].reshape(
            -1, chans
        )
        block = weight[tap * inner : (tap + 1) * inner]
        total = total + lax.dot_general(
            piece, block, (((1,), (1,)), ((), ())), preferred_element_type=jnp.float32
        )
    return total.reshape(rows, cols, -1)


def weight_grad(padded, grad_out, rows, cols):
    chans = padded.shape[2]
    flat_grad = grad_out.reshape(-1, grad_out.shape[2])
    blocks = []
    for tap in range(9):
        shift_r, shift_c = divmod(tap, 3)
        piece = padded[shift_r : shift_r + rows, shift_c : shift_c + cols].reshape(-1, chans)
        blocks.append(
            lax.dot_general(
                piece, flat_grad, (((0,), (0,)), ((), ())), preferred_element_type=jnp.float32
            )
        )
    return jnp.concatenate(blocks, 0)


def local(features, cotangent, w_first, w_second):
    rows, cols, chans = (features.shape[0], features.shape[1], features.shape[2])
    kernel_one, kernel_two = (
        lax.all_gather(w_first, ("lat", "lon"), axis=0, tiled=True),
        lax.all_gather(w_second, ("lat", "lon"), axis=0, tiled=True),
    )
    feat_pad = add_rims(features, 1)
    grad_pad = add_rims(cotangent, 1)
    pre = forward_conv(feat_pad, kernel_one, rows, cols)
    act_pad = add_rims(jax.nn.silu(pre).astype(jnp.bfloat16), 1)
    second_terms = weight_grad(act_pad, cotangent, rows, cols)
    back_act = transpose_conv(grad_pad, kernel_two, rows, cols)
    sigma = jax.nn.sigmoid(pre)
    back_pre = (back_act * sigma * (1.0 + pre * (1.0 - sigma))).astype(jnp.bfloat16)
    first_terms = weight_grad(feat_pad, back_pre, rows, cols)
    back_pad = add_rims(back_pre, 1)
    grad_features = (
        cotangent.astype(jnp.float32) + transpose_conv(back_pad, kernel_one, rows, cols)
    ).astype(jnp.bfloat16)
    grad_first, grad_second = (
        lax.psum_scatter(first_terms, ("lat", "lon"), scatter_dimension=0, tiled=True),
        lax.psum_scatter(second_terms, ("lat", "lon"), scatter_dimension=0, tiled=True),
    )
    return (grad_features, grad_first, grad_second)


def solution(mesh):
    in_specs = (
        P("lat", "lon", None),
        P("lat", "lon", None),
        P(("lat", "lon"), None),
        P(("lat", "lon"), None),
    )
    out_specs = (P("lat", "lon", None), P(("lat", "lon"), None), P(("lat", "lon"), None))
    return jax.shard_map(local, mesh=mesh, in_specs=in_specs, out_specs=out_specs, check_vma=False)
```

profile of v0, /device:TPU:1, one launch (start us, length us, event | category | flops | bytes accessed | tf_op | source)
XLA Modules:
  0.0 589.7 jit_solution(9573633949376731134)
XLA Ops:
  7.2 0.9 fusion.85
  8.1 3.1 collective-permute-start
  11.2 0.8 fusion.86
  12.0 1.8 collective-permute-start.4
  13.8 0.7 collective-permute-start.5
  14.5 179.7 %all-gather = bf16[128,9,128]{2,1,0:T(8,128)(2,1)S(1)} all-gather(bf16[1,9,128]{2,1,0:T(8,128)(2,1)} %bitcast.182), channel_id=1, replica_groups=mesh['lat'=8,'lon'=16] {'lat','lon'}, dimensions={0}, use_global_device_ids=true | all-gather | bytes 297216 | tf_op jit(solution)/shard_map/all_gather | solution.py:74
  194.3 172.1 %all-gather.1 = bf16[128,9,128]{2,1,0:T(8,128)(2,1)S(1)} all-gather(bf16[1,9,128]{2,1,0:T(8,128)(2,1)} %bitcast.183), channel_id=1, replica_groups=mesh['lat'=8,'lon'=16] {'lat','lon'}, dimensions={0}, use_global_device_ids=true | all-gather | bytes 297216 | tf_op jit(solution)/shard_map/all_gather | solution.py:73
  366.6 1.5 fusion.38
  368.2 1.5 fusion.56
  369.7 1.3 collective-permute-start.2
  371.0 4.0 collective-permute-start.3
  375.1 1.9 collective-permute-start.6
  377.0 1.5 collective-permute-start.7
  379.8 1.0 fusion.79
  382.2 1.1 fusion.81
  384.8 1.0 copy-done.3
  388.1 1.0 copy-done.2
  390.6 1.9 fusion.32
  392.5 0.8 multiply_convert_fusion
  393.3 3.2 collective-permute-start.12
  400.3 1.8 collective-permute-start.8
  402.1 1.0 collective-permute-start.9
  403.1 2.8 collective-permute-start.14
  405.9 1.3 collective-permute-start.15
  407.3 1.3 collective-permute-start.10
  408.6 4.6 collective-permute-start.11
  413.2 1.6 pad_maximum_fusion.8
  415.2 1.0 fusion.14
  416.3 1.0 fusion.13
  417.3 1.0 fusion.12
  418.4 1.1 fusion.11
  419.4 1.0 fusion.10
  420.5 1.0 fusion.9
  421.5 1.0 fusion.8
  422.6 1.0 fusion.7
  423.6 1.0 fusion.6
  425.1 1.6 fusion.78
  426.6 1.5 fusion.62
  428.2 1.4 fusion.77
  429.9 2.1 convolution_add_fusion.5
  432.4 0.7 copy-done.7
  433.2 0.5 copy-done.8
  434.1 0.8 copy-done.6
  435.2 0.8 copy-done.4
  436.7 1.1 add_convert_fusion
  437.8 142.4 %all-reduce.5.cloned.1.call-done = (f32[1152,128]{1,0:T(8,128)}, f32[1152,128]{1,0:T(8,128)}) async-done(((f32[1152,128]{1,0:T(8,128)}, f32[1152,128]{1,0:T(8,128)}), (f32[1152,128]{1,0:T(8,128)}, f32[1152,128]{1,0:T(8,128)})) %all-reduce.5.cloned.1.call-update) | async-done | bytes 1179664
  580.2 1.3 constant_dynamic-slice_fusion
  581.5 1.3 constant_dynamic-slice_fusion.1
  (79 shorter events, 15.1 us)
Async XLA Ops:
  7.2 359.5 %copy-start = (bf16[16,192,128]{2,1,0:T(8,128)(2,1)S(1)}, bf16[16,192,128]{2,1,0:T(8,128)(2,1)}, u32[]{:S(2)}) copy-start(bf16[16,192,128]{2,1,0:T(8,128)(2,1)} %param.5) | copy-start | bytes 2359300
  7.2 573.0 %all-reduce.5.cloned.1.call-start = ((), (), s32[]{:S(2)}) async-start(), calls=%async_computation | async-start | bytes 2359296
  8.1 361.6 %collective-permute-start = (bf16[16,1,128]{2,1,0:T(2,128)(2,1)S(1)}, bf16[16,1,128]{2,1,0:T(2,128)(2,1)S(1)}, u32[]{:S(2)}, u32[]{:S(2)}) collective-permute-start(bf16[16,1,128]{2,1,0:T(2,128)(2,1)S(1)} %get-tuple-element.49), channel_id=1, source_target_pairs={{0,1},{1,2},{2,3},{3,4},{4,5},{5,6},{6,7},{7,8},{8,9},{9,10},{10,1... | collective-permute-start | bytes 12296 | tf_op jit(solution)/shard_map/ppermute | solution.py:14
  11.2 358.5 %collective-permute-start.1 = (bf16[16,1,128]{2,1,0:T(2,128)(2,1)S(1)}, bf16[16,1,128]{2,1,0:T(2,128)(2,1)S(1)}, u32[]{:S(2)}, u32[]{:S(2)}) collective-permute-start(bf16[16,1,128]{2,1,0:T(2,128)(2,1)S(1)} %get-tuple-element.50), channel_id=1, source_target_pairs={{1,0},{2,1},{3,2},{4,3},{5,4},{6,5},{7,6},{8,7},{9,8},{10,9},{11,1... | collective-permute-start | bytes 12296 | tf_op jit(solution)/shard_map/ppermute | solution.py:17
  12.0 363.1 %collective-permute-start.4 = (bf16[16,1,128]{2,1,0:T(2,128)(2,1)S(1)}, bf16[16,1,128]{2,1,0:T(2,128)(2,1)S(1)}, u32[]{:S(2)}, u32[]{:S(2)}) collective-permute-start(bf16[16,1,128]{2,1,0:T(2,128)(2,1)S(1)} %get-tuple-element.53), channel_id=1, source_target_pairs={{0,1},{1,2},{2,3},{3,4},{4,5},{5,6},{6,7},{7,8},{8,9},{9,10},{10,1... | collective-permute-start | bytes 12296 | tf_op jit(solution)/shard_map/ppermute | solution.py:14
  13.8 361.3 %collective-permute-start.5 = (bf16[16,1,128]{2,1,0:T(2,128)(2,1)S(1)}, bf16[16,1,128]{2,1,0:T(2,128)(2,1)S(1)}, u32[]{:S(2)}, u32[]{:S(2)}) collective-permute-start(bf16[16,1,128]{2,1,0:T(2,128)(2,1)S(1)} %get-tuple-element.54), channel_id=1, source_target_pairs={{1,0},{2,1},{3,2},{4,3},{5,4},{6,5},{7,6},{8,7},{9,8},{10,9},{11,1... | collective-permute-start | bytes 12296 | tf_op jit(solution)/shard_map/ppermute | solution.py:17
  366.5 1.7 copy-start.1
  369.7 9.7 %collective-permute-start.2 = (bf16[1,194,128]{2,1,0:T(8,128)(2,1)S(1)}, bf16[1,194,128]{2,1,0:T(8,128)(2,1)S(1)}, u32[]{:S(2)}, u32[]{:S(2)}) collective-permute-start(bf16[1,194,128]{2,1,0:T(8,128)(2,1)S(1)} %get-tuple-element.35), channel_id=1, source_target_pairs={{16,0},{32,16},{48,32},{64,48},{80,64},{96,80},{112,96},{17,1},{33... | collective-permute-start | bytes 149000 | tf_op jit(solution)/shard_map/ppermute | solution.py:17
  371.0 8.4 %collective-permute-start.3 = (bf16[1,194,128]{2,1,0:T(8,128)(2,1)S(1)}, bf16[1,194,128]{2,1,0:T(8,128)(2,1)S(1)}, u32[]{:S(2)}, u32[]{:S(2)}) collective-permute-start(bf16[1,194,128]{2,1,0:T(8,128)(2,1)S(1)} %get-tuple-element.36), channel_id=1, source_target_pairs={{0,16},{16,32},{32,48},{48,64},{64,80},{80,96},{96,112},{1,17},{17... | collective-permute-start | bytes 149000 | tf_op jit(solution)/shard_map/ppermute | solution.py:14
  375.1 6.4 %collective-permute-start.6 = (bf16[1,194,128]{2,1,0:T(8,128)(2,1)S(1)}, bf16[1,194,128]{2,1,0:T(8,128)(2,1)S(1)}, u32[]{:S(2)}, u32[]{:S(2)}) collective-permute-start(bf16[1,194,128]{2,1,0:T(8,128)(2,1)S(1)} %get-tuple-element.39), channel_id=1, source_target_pairs={{0,16},{16,32},{32,48},{48,64},{64,80},{80,96},{96,112},{1,17},{17... | collective-permute-start | bytes 149000 | tf_op jit(solution)/shard_map/ppermute | solution.py:14
  377.0 4.9 collective-permute-start.7
  384.4 1.4 copy-start.3
  387.7 1.4 copy-start.2
  393.3 9.8 %collective-permute-start.12 = (bf16[16,1,128]{2,1,0:T(2,128)(2,1)S(1)}, bf16[16,1,128]{2,1,0:T(2,128)(2,1)S(1)}, u32[]{:S(2)}, u32[]{:S(2)}) collective-permute-start(bf16[16,1,128]{2,1,0:T(2,128)(2,1)S(1)} %get-tuple-element.41), channel_id=1, source_target_pairs={{0,1},{1,2},{2,3},{3,4},{4,5},{5,6},{6,7},{7,8},{8,9},{9,10},{10,1... | collective-permute-start | bytes 12296 | tf_op jit(solution)/shard_map/ppermute | solution.py:14
  396.5 6.6 %collective-permute-start.13 = (bf16[16,1,128]{2,1,0:T(2,128)(2,1)S(1)}, bf16[16,1,128]{2,1,0:T(2,128)(2,1)S(1)}, u32[]{:S(2)}, u32[]{:S(2)}) collective-permute-start(bf16[16,1,128]{2,1,0:T(2,128)(2,1)S(1)} %get-tuple-element.42), channel_id=1, source_target_pairs={{1,0},{2,1},{3,2},{4,3},{5,4},{6,5},{7,6},{8,7},{9,8},{10,9},{11,1... | collective-permute-start | bytes 12296 | tf_op jit(solution)/shard_map/ppermute | solution.py:17
  400.3 14.6 %copy-start.9 = (f32[1152,128]{1,0:T(8,128)}, f32[1152,128]{1,0:T(8,128)S(1)}, u32[]{:S(2)}) copy-start(f32[1152,128]{1,0:T(8,128)S(1)} %fusion.15) | copy-start | bytes 1769476
  400.3 6.9 %collective-permute-start.8 = (bf16[16,1,128]{2,1,0:T(2,128)(2,1)S(1)}, bf16[16,1,128]{2,1,0:T(2,128)(2,1)S(1)}, u32[]{:S(2)}, u32[]{:S(2)}) collective-permute-start(bf16[16,1,128]{2,1,0:T(2,128)(2,1)S(1)} %get-tuple-element.45), channel_id=1, source_target_pairs={{0,1},{1,2},{2,3},{3,4},{4,5},{5,6},{6,7},{7,8},{8,9},{9,10},{10,1... | collective-permute-start | bytes 12296 | tf_op jit(solution)/shard_map/ppermute | solution.py:14
  402.1 5.1 collective-permute-start.9
  403.1 11.7 %collective-permute-start.14 = (bf16[1,194,128]{2,1,0:T(8,128)(2,1)S(1)}, bf16[1,194,128]{2,1,0:T(8,128)(2,1)S(1)}, u32[]{:S(2)}, u32[]{:S(2)}) collective-permute-start(bf16[1,194,128]{2,1,0:T(8,128)(2,1)S(1)} %get-tuple-element.28), channel_id=1, source_target_pairs={{0,16},{16,32},{32,48},{48,64},{64,80},{80,96},{96,112},{1,17},{17... | collective-permute-start | bytes 149000 | tf_op jit(solution)/shard_map/ppermute | solution.py:14
  405.9 8.9 %collective-permute-start.15 = (bf16[1,194,128]{2,1,0:T(8,128)(2,1)S(1)}, bf16[1,194,128]{2,1,0:T(8,128)(2,1)S(1)}, u32[]{:S(2)}, u32[]{:S(2)}) collective-permute-start(bf16[1,194,128]{2,1,0:T(8,128)(2,1)S(1)} %get-tuple-element.27), channel_id=1, source_target_pairs={{16,0},{32,16},{48,32},{64,48},{80,64},{96,80},{112,96},{17,1},{33... | collective-permute-start | bytes 149000 | tf_op jit(solution)/shard_map/ppermute | solution.py:17
  407.3 17.4 %collective-permute-start.10 = (bf16[1,194,128]{2,1,0:T(8,128)(2,1)S(1)}, bf16[1,194,128]{2,1,0:T(8,128)(2,1)S(1)}, u32[]{:S(2)}, u32[]{:S(2)}) collective-permute-start(bf16[1,194,128]{2,1,0:T(8,128)(2,1)S(1)} %get-tuple-element.31), channel_id=1, source_target_pairs={{16,0},{32,16},{48,32},{64,48},{80,64},{96,80},{112,96},{17,1},{33... | collective-permute-start | bytes 149000 | tf_op jit(solution)/shard_map/ppermute | solution.py:17
  408.6 16.1 %collective-permute-start.11 = (bf16[1,194,128]{2,1,0:T(8,128)(2,1)S(1)}, bf16[1,194,128]{2,1,0:T(8,128)(2,1)S(1)}, u32[]{:S(2)}, u32[]{:S(2)}) collective-permute-start(bf16[1,194,128]{2,1,0:T(8,128)(2,1)S(1)} %get-tuple-element.32), channel_id=1, source_target_pairs={{0,16},{16,32},{32,48},{48,64},{64,80},{80,96},{96,112},{1,17},{17... | collective-permute-start | bytes 149000 | tf_op jit(solution)/shard_map/ppermute | solution.py:14
  429.9 2.1 copy-start.5
  432.0 1.1 copy-start.7
  432.0 1.6 copy-start.8
  433.7 1.1 copy-start.6
  434.8 1.1 copy-start.4
Sparse Core Ops, SparseCore 0:
  430.0 150.1 all-reduce.4
where the time goes:
time: 590 us
  blocking collectives  352 us (60%)
  waiting for transfers between devices  143 us (24%)
  starting transfers between devices  30.3 us (5%)
  matrix products  29.7 us (5%)
  between operations  14.5 us (2%)
  local copies, waits for them, and re-layouts  14.4 us (2%)
  other arithmetic  6.05 us (1%)
    all_gather x1, blocking collectives, local(): lax.all_gather(w_second, ('lat', 'lon'), axis=0, tiled=True)  180 us
    all_gather x1, blocking collectives, local(): lax.all_gather(w_first, ('lat', 'lon'), axis=0, tiled=True)  172 us
    unnamed x2, waiting for transfers between devices  142 us
    ppermute x8, starting transfers between devices, padded_2(): lax.ppermute(lax.slice_in_dim(block, block.shape[dim] - width, None, axis...  23.2 us
    dot_general x18, matrix products, weight_grad(): lax.dot_general(piece, flat_grad, (((0,), (0,)), ((), ())), preferred_ele...  13.2 us
    dot_general x18, matrix products, transpose_conv(): lax.dot_general(piece, block, (((1,), (1,)), ((), ())), preferred_element...  12.2 us
  transfers between devices with their start and end apart: 17, of which 2 were waited for; matrix products, arithmetic and copies ran while one was open for 5% of the time, Pallas kernels for 0%

commit v1 on v0

--- a/solution.py
+++ b/solution.py
@@ -2,6 +2,7 @@
 import jax.numpy as jnp
 from jax import lax
 from jax.sharding import PartitionSpec as P
+from jax.lax import all_to_all, axis_size
 
 
 def padded_2(block, sides, width, periodic):
@@ -69,8 +70,16 @@
 
 def local(features, cotangent, w_first, w_second):
     rows, cols, chans = (features.shape[0], features.shape[1], features.shape[2])
+
+    def drive_pages(x_local):
+        t_next = axis_size(("lat", "lon"))
+        taken_in = jnp.stack(t_next * [x_local])
+        current_block = all_to_all(taken_in, axis_name=("lat", "lon"), split_axis=0, concat_axis=0)
+        vec_out = jnp.concatenate(current_block, axis=0)
+        return vec_out
+
     kernel_one, kernel_two = (
-        lax.all_gather(w_first, ("lat", "lon"), axis=0, tiled=True),
+        drive_pages(w_first),
         lax.all_gather(w_second, ("lat", "lon"), axis=0, tiled=True),
     )
     feat_pad = add_rims(features, 1)

time: 590 us -> 442 us (0.75)
  blocking collectives: 352 us -> 180 us
  starting transfers between devices: 30.3 us -> 42.2 us
  local copies, waits for them, and re-layouts: 14.4 us -> 24.6 us
    all_gather x1 -> x0, blocking collectives: 172 us -> none  [local(): lax.all_gather(w_first, ('lat', 'lon'), axis=0, tiled=True)]
    all_to_all x0 -> x1, starting transfers between devices: none -> 11.6 us  [drive_pages(): all_to_all(taken_in, axis_name=('lat', 'lon'), split_axis=0, concat_axis=0)]
    unnamed x24 -> x47, local copies, waits for them, and re-layouts: 7.77 us -> 13.4 us
  transfers between devices with their start and end apart: 17 -> 18, of which waited for: 2 -> 1; matrix products, arithmetic and copies ran while one was open for 5% -> 8% of each run, Pallas kernels for 0% -> 0%
where the time goes in v1:
time: 442 us; the launch traced here: 441 us
  blocking collectives  180 us (41%)
  waiting for transfers between devices  142 us (32%)
  starting transfers between devices  42.2 us (10%)
  matrix products  30.8 us (7%)
  local copies, waits for them, and re-layouts  24.6 us (6%)
  between operations  14.6 us (3%)
  other arithmetic  6.86 us (2%)
    all_gather x1, blocking collectives, local(): lax.all_gather(w_second, ('lat', 'lon'), axis=0, tiled=True)  180 us
    unnamed x2, waiting for transfers between devices  142 us
    ppermute x8, starting transfers between devices, padded_2(): lax.ppermute(lax.slice_in_dim(block, block.shape[dim] - width, None, axis...  20.9 us
    unnamed x47, local copies, waits for them, and re-layouts  13.4 us
    dot_general x18, matrix products, transpose_conv(): lax.dot_general(piece, block, (((1,), (1,)), ((), ())), preferred_element...  13.4 us
    dot_general x18, matrix products, weight_grad(): lax.dot_general(piece, flat_grad, (((0,), (0,)), ((), ())), preferred_ele...  13.1 us
    all_to_all x1, starting transfers between devices, drive_pages(): all_to_all(taken_in, axis_name=('lat', 'lon'), split_axis=0, concat_axis=0)  11.6 us
    ppermute x8, starting transfers between devices, padded_2(): lax.ppermute(lax.slice_in_dim(block, 0, width, axis=dim), axis, backward)  9.69 us
  transfers between devices with their start and end apart: 18, of which 1 were waited for; matrix products, arithmetic and copies ran while one was open for 8% of the time, Pallas kernels for 0%

profile of v1, /device:TPU:1, one launch (start us, length us, event | category | flops | bytes accessed | tf_op | source)
XLA Modules:
  0.0 440.5 jit_solution(14837902452169304346)
XLA Ops:
  7.2 0.9 fusion.85
  8.1 3.1 collective-permute-start
  11.1 0.8 fusion.86
  11.9 1.8 collective-permute-start.4
  14.5 1.5 stack.2
  16.0 11.6 %all-to-all-start = ((bf16[128,9,128]{2,1,0:T(8,128)(2,1)}), bf16[128,9,128]{2,1,0:T(8,128)(2,1)}, u32[]{:S(2)}, u32[]{:S(2)}) async-start(bf16[128,9,128]{2,1,0:T(8,128)(2,1)} %stack.2), calls=%async_computation | async-start | bytes 1048576 | tf_op jit(solution)/shard_map/all_to_all | solution.py:77
  27.7 179.7 %all-gather = bf16[128,9,128]{2,1,0:T(8,128)(2,1)S(1)} all-gather(bf16[1,9,128]{2,1,0:T(8,128)(2,1)S(1)} %bitcast.181), channel_id=1, replica_groups=mesh['lat'=8,'lon'=16] {'lat','lon'}, dimensions={0}, use_global_device_ids=true | all-gather | bytes 297216 | tf_op jit(solution)/shard_map/all_gather | solution.py:83
  207.6 1.5 fusion.38
  209.2 1.3 collective-permute-start.2
  210.5 4.0 collective-permute-start.3
  214.5 1.9 collective-permute-start.6
  216.5 1.5 collective-permute-start.7
  218.4 1.3 pad_maximum_fusion.10
  220.1 0.9 fusion.79
  222.5 1.0 copy-done.7
  225.1 2.7 fusion.81
  227.8 1.6 convolution_add_fusion.12
  229.3 1.2 reshape.130
  230.5 1.5 fusion.64
  235.0 0.8 copy-done.6
  238.9 1.0 copy-done.8
  239.9 1.9 fusion.32
  242.7 1.0 collective-permute-start.13
  247.8 0.9 copy-done.20
  248.7 1.1 collective-permute-start.8
  249.7 2.6 collective-permute-start.9
  252.4 4.3 collective-permute-start.14
  256.7 1.3 collective-permute-start.15
  258.1 1.3 collective-permute-start.10
  259.4 4.6 %collective-permute-start.11 = (bf16[1,194,128]{2,1,0:T(8,128)(2,1)S(1)}, bf16[1,194,128]{2,1,0:T(8,128)(2,1)S(1)}, u32[]{:S(2)}, u32[]{:S(2)}) collective-permute-start(bf16[1,194,128]{2,1,0:T(8,128)(2,1)S(1)} %get-tuple-element.32), channel_id=1, source_target_pairs={{0,16},{16,32},{32,48},{48,64},{64,80},{80,96},{96,112},{1,17},{17... | collective-permute-start | bytes 149000 | tf_op jit(solution)/shard_map/ppermute | solution.py:15
  264.0 1.6 pad_maximum_fusion.8
  266.0 1.0 fusion.14
  267.1 1.0 fusion.13
  268.1 1.0 fusion.12
  269.1 1.0 fusion.11
  270.2 1.0 fusion.10
  271.2 1.1 fusion.9
  272.3 1.0 fusion.8
  273.3 1.0 fusion.7
  274.4 1.0 fusion.6
  275.8 1.6 fusion.78
  277.4 1.5 fusion.62
  278.9 1.5 fusion.77
  280.8 2.1 convolution_add_fusion.5
  288.3 1.1 add_convert_fusion
  289.4 141.7 %all-reduce.5.cloned.1.call-done = (f32[1152,128]{1,0:T(8,128)}, f32[1152,128]{1,0:T(8,128)}) async-done(((f32[1152,128]{1,0:T(8,128)}, f32[1152,128]{1,0:T(8,128)}), (f32[1152,128]{1,0:T(8,128)}, f32[1152,128]{1,0:T(8,128)})) %all-reduce.5.cloned.1.call-update) | async-done | bytes 1179664
  431.0 1.3 constant_dynamic-slice_fusion
  432.4 1.3 constant_dynamic-slice_fusion.1
  (105 shorter events, 22.3 us)
Async XLA Ops:
  7.2 200.4 %copy-start = (bf16[16,192,128]{2,1,0:T(8,128)(2,1)S(1)}, bf16[16,192,128]{2,1,0:T(8,128)(2,1)}, u32[]{:S(2)}) copy-start(bf16[16,192,128]{2,1,0:T(8,128)(2,1)} %param.5) | copy-start | bytes 2359300
  7.2 20.5 %copy-start.21 = (bf16[9,128]{1,0:T(8,128)(2,1)S(1)}, bf16[9,128]{1,0:T(8,128)(2,1)}, u32[]{:S(2)}) copy-start(bf16[9,128]{1,0:T(8,128)(2,1)} %param.7) | copy-start | bytes 6916
  8.1 201.1 %collective-permute-start = (bf16[16,1,128]{2,1,0:T(2,128)(2,1)S(1)}, bf16[16,1,128]{2,1,0:T(2,128)(2,1)S(1)}, u32[]{:S(2)}, u32[]{:S(2)}) collective-permute-start(bf16[16,1,128]{2,1,0:T(2,128)(2,1)S(1)} %get-tuple-element.49), channel_id=1, source_target_pairs={{0,1},{1,2},{2,3},{3,4},{4,5},{5,6},{6,7},{7,8},{8,9},{9,10},{10,1... | collective-permute-start | bytes 12296 | tf_op jit(solution)/shard_map/ppermute | solution.py:15
  11.1 198.0 %collective-permute-start.1 = (bf16[16,1,128]{2,1,0:T(2,128)(2,1)S(1)}, bf16[16,1,128]{2,1,0:T(2,128)(2,1)S(1)}, u32[]{:S(2)}, u32[]{:S(2)}) collective-permute-start(bf16[16,1,128]{2,1,0:T(2,128)(2,1)S(1)} %get-tuple-element.50), channel_id=1, source_target_pairs={{1,0},{2,1},{3,2},{4,3},{5,4},{6,5},{7,6},{8,7},{9,8},{10,9},{11,1... | collective-permute-start | bytes 12296 | tf_op jit(solution)/shard_map/ppermute | solution.py:18
  11.9 202.5 %collective-permute-start.4 = (bf16[16,1,128]{2,1,0:T(2,128)(2,1)S(1)}, bf16[16,1,128]{2,1,0:T(2,128)(2,1)S(1)}, u32[]{:S(2)}, u32[]{:S(2)}) collective-permute-start(bf16[16,1,128]{2,1,0:T(2,128)(2,1)S(1)} %get-tuple-element.53), channel_id=1, source_target_pairs={{0,1},{1,2},{2,3},{3,4},{4,5},{5,6},{6,7},{7,8},{8,9},{9,10},{10,1... | collective-permute-start | bytes 12296 | tf_op jit(solution)/shard_map/ppermute | solution.py:15
  13.7 200.7 %collective-permute-start.5 = (bf16[16,1,128]{2,1,0:T(2,128)(2,1)S(1)}, bf16[16,1,128]{2,1,0:T(2,128)(2,1)S(1)}, u32[]{:S(2)}, u32[]{:S(2)}) collective-permute-start(bf16[16,1,128]{2,1,0:T(2,128)(2,1)S(1)} %get-tuple-element.54), channel_id=1, source_target_pairs={{1,0},{2,1},{3,2},{4,3},{5,4},{6,5},{7,6},{8,7},{9,8},{10,9},{11,1... | collective-permute-start | bytes 12296 | tf_op jit(solution)/shard_map/ppermute | solution.py:18
  16.0 213.3 %all-to-all-start = ((bf16[128,9,128]{2,1,0:T(8,128)(2,1)}), bf16[128,9,128]{2,1,0:T(8,128)(2,1)}, u32[]{:S(2)}, u32[]{:S(2)}) async-start(bf16[128,9,128]{2,1,0:T(8,128)(2,1)} %stack.2), calls=%async_computation | async-start | bytes 1048576 | tf_op jit(solution)/shard_map/all_to_all | solution.py:77
  27.6 403.4 %all-reduce.5.cloned.1.call-start = ((), (), s32[]{:S(2)}) async-start(), calls=%async_computation.1 | async-start | bytes 2359296
  207.6 6.9 %copy-start.1 = (bf16[16,192,128]{2,1,0:T(8,128)(2,1)S(1)}, bf16[16,192,128]{2,1,0:T(8,128)(2,1)}, u32[]{:S(2)}) copy-start(bf16[16,192,128]{2,1,0:T(8,128)(2,1)} %param.4) | copy-start | bytes 2359300
  209.2 10.5 %collective-permute-start.2 = (bf16[1,194,128]{2,1,0:T(8,128)(2,1)S(1)}, bf16[1,194,128]{2,1,0:T(8,128)(2,1)S(1)}, u32[]{:S(2)}, u32[]{:S(2)}) collective-permute-start(bf16[1,194,128]{2,1,0:T(8,128)(2,1)S(1)} %get-tuple-element.35), channel_id=1, source_target_pairs={{16,0},{32,16},{48,32},{64,48},{80,64},{96,80},{112,96},{17,1},{33... | collective-permute-start | bytes 149000 | tf_op jit(solution)/shard_map/ppermute | solution.py:18
  210.5 9.2 %collective-permute-start.3 = (bf16[1,194,128]{2,1,0:T(8,128)(2,1)S(1)}, bf16[1,194,128]{2,1,0:T(8,128)(2,1)S(1)}, u32[]{:S(2)}, u32[]{:S(2)}) collective-permute-start(bf16[1,194,128]{2,1,0:T(8,128)(2,1)S(1)} %get-tuple-element.36), channel_id=1, source_target_pairs={{0,16},{16,32},{32,48},{48,64},{64,80},{80,96},{96,112},{1,17},{17... | collective-permute-start | bytes 149000 | tf_op jit(solution)/shard_map/ppermute | solution.py:15
  214.5 10.1 %collective-permute-start.6 = (bf16[1,194,128]{2,1,0:T(8,128)(2,1)S(1)}, bf16[1,194,128]{2,1,0:T(8,128)(2,1)S(1)}, u32[]{:S(2)}, u32[]{:S(2)}) collective-permute-start(bf16[1,194,128]{2,1,0:T(8,128)(2,1)S(1)} %get-tuple-element.39), channel_id=1, source_target_pairs={{0,16},{16,32},{32,48},{48,64},{64,80},{80,96},{96,112},{1,17},{17... | collective-permute-start | bytes 149000 | tf_op jit(solution)/shard_map/ppermute | solution.py:15
  216.5 8.2 %collective-permute-start.7 = (bf16[1,194,128]{2,1,0:T(8,128)(2,1)S(1)}, bf16[1,194,128]{2,1,0:T(8,128)(2,1)S(1)}, u32[]{:S(2)}, u32[]{:S(2)}) collective-permute-start(bf16[1,194,128]{2,1,0:T(8,128)(2,1)S(1)} %get-tuple-element.40), channel_id=1, source_target_pairs={{16,0},{32,16},{48,32},{64,48},{80,64},{96,80},{112,96},{17,1},{33... | collective-permute-start | bytes 149000 | tf_op jit(solution)/shard_map/ppermute | solution.py:18
  219.7 16.6 %copy-start.4 = (bf16[16,192,128]{2,1,0:T(8,128)(2,1)}, bf16[16,192,128]{2,1,0:T(8,128)(2,1)S(1)}, u32[]{:S(2)}) copy-start(bf16[16,192,128]{2,1,0:T(8,128)(2,1)S(1)} %get-tuple-element.51) | copy-start | bytes 2359300
  222.1 1.4 copy-start.7
  225.1 2.7 copy-start.2
  232.0 1.1 copy-start.9
  232.4 1.2 copy-start.16
  233.5 1.1 copy-start.15
  234.7 1.1 copy-start.6
  236.3 1.1 copy-start.12
  237.4 1.1 copy-start.10
  238.5 1.4 copy-start.8
  241.8 1.9 copy-start.3
  242.6 9.7 %collective-permute-start.12 = (bf16[16,1,128]{2,1,0:T(2,128)(2,1)S(1)}, bf16[16,1,128]{2,1,0:T(2,128)(2,1)S(1)}, u32[]{:S(2)}, u32[]{:S(2)}) collective-permute-start(bf16[16,1,128]{2,1,0:T(2,128)(2,1)S(1)} %get-tuple-element.41), channel_id=1, source_target_pairs={{0,1},{1,2},{2,3},{3,4},{4,5},{5,6},{6,7},{7,8},{8,9},{9,10},{10,1... | collective-permute-start | bytes 12296 | tf_op jit(solution)/shard_map/ppermute | solution.py:15
  242.7 9.7 %collective-permute-start.13 = (bf16[16,1,128]{2,1,0:T(2,128)(2,1)S(1)}, bf16[16,1,128]{2,1,0:T(2,128)(2,1)S(1)}, u32[]{:S(2)}, u32[]{:S(2)}) collective-permute-start(bf16[16,1,128]{2,1,0:T(2,128)(2,1)S(1)} %get-tuple-element.42), channel_id=1, source_target_pairs={{1,0},{2,1},{3,2},{4,3},{5,4},{6,5},{7,6},{8,7},{9,8},{10,9},{11,1... | collective-permute-start | bytes 12296 | tf_op jit(solution)/shard_map/ppermute | solution.py:18
  245.0 1.1 copy-start.5
  247.8 0.9 copy-start.20
  248.7 9.4 %collective-permute-start.8 = (bf16[16,1,128]{2,1,0:T(2,128)(2,1)S(1)}, bf16[16,1,128]{2,1,0:T(2,128)(2,1)S(1)}, u32[]{:S(2)}, u32[]{:S(2)}) collective-permute-start(bf16[16,1,128]{2,1,0:T(2,128)(2,1)S(1)} %get-tuple-element.45), channel_id=1, source_target_pairs={{0,1},{1,2},{2,3},{3,4},{4,5},{5,6},{6,7},{7,8},{8,9},{9,10},{10,1... | collective-permute-start | bytes 12296 | tf_op jit(solution)/shard_map/ppermute | solution.py:15
  249.7 8.3 %collective-permute-start.9 = (bf16[16,1,128]{2,1,0:T(2,128)(2,1)S(1)}, bf16[16,1,128]{2,1,0:T(2,128)(2,1)S(1)}, u32[]{:S(2)}, u32[]{:S(2)}) collective-permute-start(bf16[16,1,128]{2,1,0:T(2,128)(2,1)S(1)} %get-tuple-element.46), channel_id=1, source_target_pairs={{1,0},{2,1},{3,2},{4,3},{5,4},{6,5},{7,6},{8,7},{9,8},{10,9},{11,1... | collective-permute-start | bytes 12296 | tf_op jit(solution)/shard_map/ppermute | solution.py:18
  252.4 13.2 %collective-permute-start.14 = (bf16[1,194,128]{2,1,0:T(8,128)(2,1)S(1)}, bf16[1,194,128]{2,1,0:T(8,128)(2,1)S(1)}, u32[]{:S(2)}, u32[]{:S(2)}) collective-permute-start(bf16[1,194,128]{2,1,0:T(8,128)(2,1)S(1)} %get-tuple-element.28), channel_id=1, source_target_pairs={{0,16},{16,32},{32,48},{48,64},{64,80},{80,96},{96,112},{1,17},{17... | collective-permute-start | bytes 149000 | tf_op jit(solution)/shard_map/ppermute | solution.py:15
  256.7 8.9 %collective-permute-start.15 = (bf16[1,194,128]{2,1,0:T(8,128)(2,1)S(1)}, bf16[1,194,128]{2,1,0:T(8,128)(2,1)S(1)}, u32[]{:S(2)}, u32[]{:S(2)}) collective-permute-start(bf16[1,194,128]{2,1,0:T(8,128)(2,1)S(1)} %get-tuple-element.27), channel_id=1, source_target_pairs={{16,0},{32,16},{48,32},{64,48},{80,64},{96,80},{112,96},{17,1},{33... | collective-permute-start | bytes 149000 | tf_op jit(solution)/shard_map/ppermute | solution.py:18
  258.1 17.3 %collective-permute-start.10 = (bf16[1,194,128]{2,1,0:T(8,128)(2,1)S(1)}, bf16[1,194,128]{2,1,0:T(8,128)(2,1)S(1)}, u32[]{:S(2)}, u32[]{:S(2)}) collective-permute-start(bf16[1,194,128]{2,1,0:T(8,128)(2,1)S(1)} %get-tuple-element.31), channel_id=1, source_target_pairs={{16,0},{32,16},{48,32},{64,48},{80,64},{96,80},{112,96},{17,1},{33... | collective-permute-start | bytes 149000 | tf_op jit(solution)/shard_map/ppermute | solution.py:18
  259.4 16.0 %collective-permute-start.11 = (bf16[1,194,128]{2,1,0:T(8,128)(2,1)S(1)}, bf16[1,194,128]{2,1,0:T(8,128)(2,1)S(1)}, u32[]{:S(2)}, u32[]{:S(2)}) collective-permute-start(bf16[1,194,128]{2,1,0:T(8,128)(2,1)S(1)} %get-tuple-element.32), channel_id=1, source_target_pairs={{0,16},{16,32},{32,48},{48,64},{64,80},{80,96},{96,112},{1,17},{17... | collective-permute-start | bytes 149000 | tf_op jit(solution)/shard_map/ppermute | solution.py:15
  280.8 2.1 copy-start.14
  282.9 1.1 copy-start.18
  282.9 1.6 copy-start.19
  284.6 1.1 copy-start.17
  285.7 1.1 copy-start.13
  286.8 1.1 copy-start.11
Sparse Core Ops, SparseCore 0:
  280.9 150.0 all-reduce.4
